TPU v7x, 512 devices: a whole 4x4x16 slice. The times are simulated.
512 devices in a mesh: tile: 64 (over x, z_lo, core), tm: 8 (over z_hi, y).
Axes of the slice: x: 4, y: 4, z: 16 (z_hi: 2, z_lo: 8; z = z_hi * 8 + z_lo), core: 2. Of those that a mesh axis runs over, the one named last changes fastest.
Arguments:
- controls: float32 [16, 512, 8, 512], P('tm', 'tile'), may hold values from -6 to 6
- perturbations: bfloat16 [8, 16, 4, 512, 8, 512], P('tm', None, None, 'tile'), may hold values from -6 to 6
- owner: int32 [16], replicated, may hold values from 0 to 15, each once
- land_mask: int32 [512, 512], P('tile'), may hold values 0 or 1
- diffusivity: float32 [2, 8], replicated, may hold values from 0.2 to 0.24
Outputs:
- increment: float32 [8, 4, 512, 8, 512], P('tm', None, 'tile')
Inputs may be any that keep to these rules, and one draw needn't show every extreme that they name: owner names every member exactly once.
All inputs are finite; a program needn't handle non-finite values. No bound on the sum of `land_mask` on one device may be relied on, other than what follows from the above.
Results may differ from a plain program's by a relative error of at most 0.0029.
Values may be sent and summed in bfloat16 or wider, within the bound.
A program may use at most 64 MiB of HBM per device.

v0:
```python
import math
import jax
import jax.numpy as jnp
from jax import lax
from jax.sharding import PartitionSpec as P

SWEEPS = 4


def halo_rows(cells, width, dim):
    count = lax.axis_size("tile")
    ends = count - 1
    head = lax.slice_in_dim(cells, 0, width, axis=dim)
    tail = lax.slice_in_dim(cells, cells.shape[dim] - width, cells.shape[dim], axis=dim)
    before = lax.ppermute(tail, "tile", [(i, i + 1) for i in range(ends)])
    after = lax.ppermute(head, "tile", [(i + 1, i) for i in range(ends)])
    return jnp.concatenate([before, cells, after], axis=dim)


def weight_sweep(field, coef):
    padded = jnp.pad(field, ((0, 0), (1, 1), (0, 0), (1, 1)))
    coef_pad = jnp.pad(coef, ((1, 1), (0, 0), (1, 1)))
    flux = 0.5 * (coef + coef_pad[:-2, :, 1:-1]) * (padded[:, :-2, :, 1:-1] - field)
    flux = flux + 0.5 * (coef + coef_pad[2:, :, 1:-1]) * (padded[:, 2:, :, 1:-1] - field)
    flux = flux + 0.5 * (coef + coef_pad[1:-1, :, :-2]) * (padded[:, 1:-1, :, :-2] - field)
    flux = flux + 0.5 * (coef + coef_pad[1:-1, :, 2:]) * (padded[:, 1:-1, :, 2:] - field)
    return field + flux


def on_device(controls, perturbations, owner, land_mask, diffusivity):
    rows = controls.shape[1]
    width = SWEEPS
    tile = lax.axis_index("tile")
    count = lax.axis_size("tile")
    grow = tile * rows - width + jnp.arange(rows + 2 * width)
    inside = (grow >= 0) & (grow < count * rows)
    mask_wide = halo_rows(land_mask, width, 0)
    coef = jnp.where(
        mask_wide[:, None, :] == 1, diffusivity[1][None, :, None], diffusivity[0][None, :, None]
    )
    coef = jnp.where(inside[:, None, None], coef, 0.0)
    keep = inside[None, :, None, None]
    smooth = jnp.where(keep, halo_rows(controls, width, 1), 0.0)
    for sweep_index in range(SWEEPS):
        smooth = jnp.where(keep, weight_sweep(smooth, coef), 0.0)
    weights = smooth[:, width : width + rows].astype(jnp.bfloat16)
    every = lax.all_gather(weights, "tm", axis=0, tiled=True)
    by_member = jnp.zeros_like(every).at[owner].set(every)
    member_count = owner.shape[0]
    factor = 1.0 / math.sqrt(member_count - 1)
    summed = jnp.einsum(
        "mvxly,mxly->vxly", perturbations[0], by_member, preferred_element_type=jnp.float32
    )
    return (summed * factor)[None]


def solution(mesh):
    return jax.shard_map(
        on_device,
        mesh=mesh,
        in_specs=(
            P("tm", "tile", None, None),
            P("tm", None, None, "tile", None, None),
            P(),
            P("tile", None),
            P(),
        ),
        out_specs=P("tm", None, "tile", None, None),
        check_vma=False,
    )
```

profile of v0, /device:TPU:2, one launch (start us, length us, event | category | flops | bytes accessed | tf_op | source)
XLA Modules:
  0.0 150.7 jit_solution(17457148186831489938)
XLA Ops:
  6.5 0.0 all-gather.2.cloned.1.call-start
  6.5 0.8 fusion.59
  7.3 1.9 %collective-permute-start.2 = (s32[4,512]{1,0:T(4,128)S(1)}, s32[4,512]{1,0:T(4,128)S(1)}, u32[]{:S(2)}, u32[]{:S(2)}) collective-permute-start(s32[4,512]{1,0:T(4,128)S(1)} %get-tuple-element.15), channel_id=1, source_target_pairs={{0,8},{8,16},{16,24},{24,32},{32,40},{40,48},{48,56},{56,64},{64,7... | collective-permute-start | bytes 24584 | tf_op jit(solution)/shard_map/ppermute | solution.py:15
  9.3 12.6 %collective-permute-start.3 = (s32[4,512]{1,0:T(4,128)S(1)}, s32[4,512]{1,0:T(4,128)S(1)}, u32[]{:S(2)}, u32[]{:S(2)}) collective-permute-start(s32[4,512]{1,0:T(4,128)S(1)} %get-tuple-element.16), channel_id=1, source_target_pairs={{8,0},{16,8},{24,16},{32,24},{40,32},{48,40},{56,48},{64,56},{72,6... | collective-permute-start | bytes 24584 | tf_op jit(solution)/shard_map/ppermute | solution.py:16
  21.8 1.0 fusion.58
  22.8 1.9 %collective-permute-start = (f32[2,4,8,512]{3,2,1,0:T(8,128)S(1)}, f32[2,4,8,512]{3,2,1,0:T(8,128)S(1)}, u32[]{:S(2)}, u32[]{:S(2)}) collective-permute-start(f32[2,4,8,512]{3,2,1,0:T(8,128)S(1)} %get-tuple-element.13), channel_id=1, source_target_pairs={{0,8},{8,16},{16,24},{24,32},{32,40},{40,48},{48,56},{56,64},{64,7... | collective-permute-start | bytes 393224 | tf_op jit(solution)/shard_map/ppermute | solution.py:15
  24.8 11.1 %collective-permute-start.1 = (f32[2,4,8,512]{3,2,1,0:T(8,128)S(1)}, f32[2,4,8,512]{3,2,1,0:T(8,128)S(1)}, u32[]{:S(2)}, u32[]{:S(2)}) collective-permute-start(f32[2,4,8,512]{3,2,1,0:T(8,128)S(1)} %get-tuple-element.14), channel_id=1, source_target_pairs={{8,0},{16,8},{24,16},{32,24},{40,32},{48,40},{56,48},{64,56},{72,6... | collective-permute-start | bytes 393224 | tf_op jit(solution)/shard_map/ppermute | solution.py:16
  35.9 0.8 slice_bitcast_fusion.1
  36.7 0.1 slice.128
  36.8 0.0 collective-permute-done.2
  36.8 0.0 collective-permute-done.3
  36.8 0.7 add_compare_fusion
  37.5 0.1 select_select_fusion
  37.6 0.2 fusion.45
  37.9 0.0 collective-permute-done
  37.9 0.5 collective-permute-done.1
  38.4 1.0 maximum_select_fusion
  39.5 0.4 fusion.6
  39.9 0.0 copy-start
  39.9 0.4 fusion.19
  40.3 0.4 fusion.32
  40.6 0.3 fusion.40
  41.0 0.8 fusion.56
  41.7 0.0 all-gather.2.cloned.1.call-update
  41.8 0.0 copy-done
  41.8 95.4 %all-gather.2.cloned.1.call-done = bf16[16,8,8,512]{3,2,1,0:T(8,128)(2,1)} async-done(((bf16[2,8,8,512]{3,2,1,0:T(8,128)(2,1)}), bf16[16,8,8,512]{3,2,1,0:T(8,128)(2,1)}) %all-gather.2.cloned.1.call-update) | async-done | bytes 1048592 | tf_op jit(solution)/shard_map/all_gather | solution.py:47
  137.2 0.1 broadcast_in_dim.96
  137.3 2.3 %scatter_fusion = bf16[16,8,8,512]{3,2,1,0:T(8,128)(2,1)S(1)} fusion(bf16[16,8,8,512]{3,2,1,0:T(8,128)(2,1)S(1)} %broadcast_in_dim.96, s32[16]{0:T(128)S(1)} %compare_select_fusion, bf16[16,8,8,512]{3,2,1,0:T(8,128)(2,1)} %all-gather.2.cloned.1.call-done), kind=kCustom, calls=%fused_computation | custom fusion | bytes 3145792 | tf_op jit(solution)/shard_map/scatter | solution.py:48
  139.6 0.3 bitcast_convert_fusion
  139.8 3.2 %multiply_reduce_fusion = f32[8,8,512,4]{2,1,0,3:T(8,128)S(1)} fusion(f32[8,8,512,16]{2,1,0,3:T(8,128)S(1)} %bitcast_convert_fusion, bf16[1,16,4,8,8,512]{5,4,3,2,1,0:T(8,128)(2,1)} %param.6), kind=kLoop, calls=%fused_computation.1 | loop fusion | flops 6160384 | bytes 6815744 | tf_op jit(solution)/shard_map/mvxly,mxly->vxly/dot_general | solution.py:51
  143.0 0.8 multiply_bitcast_fusion
  (4 shorter events, 0.0 us)
Async XLA Ops:
  6.5 130.7 %all-gather.2.cloned.1.call-start = ((), (), s32[]{:S(2)}) async-start(), calls=%async_computation | async-start | bytes 1179648 | tf_op jit(solution)/shard_map/all_gather | solution.py:47
  7.3 29.4 %collective-permute-start.2 = (s32[4,512]{1,0:T(4,128)S(1)}, s32[4,512]{1,0:T(4,128)S(1)}, u32[]{:S(2)}, u32[]{:S(2)}) collective-permute-start(s32[4,512]{1,0:T(4,128)S(1)} %get-tuple-element.15), channel_id=1, source_target_pairs={{0,8},{8,16},{16,24},{24,32},{32,40},{40,48},{48,56},{56,64},{64,7... | collective-permute-start | bytes 24584 | tf_op jit(solution)/shard_map/ppermute | solution.py:15
  9.3 27.5 %collective-permute-start.3 = (s32[4,512]{1,0:T(4,128)S(1)}, s32[4,512]{1,0:T(4,128)S(1)}, u32[]{:S(2)}, u32[]{:S(2)}) collective-permute-start(s32[4,512]{1,0:T(4,128)S(1)} %get-tuple-element.16), channel_id=1, source_target_pairs={{8,0},{16,8},{24,16},{32,24},{40,32},{48,40},{56,48},{64,56},{72,6... | collective-permute-start | bytes 24584 | tf_op jit(solution)/shard_map/ppermute | solution.py:16
  22.8 15.0 %collective-permute-start = (f32[2,4,8,512]{3,2,1,0:T(8,128)S(1)}, f32[2,4,8,512]{3,2,1,0:T(8,128)S(1)}, u32[]{:S(2)}, u32[]{:S(2)}) collective-permute-start(f32[2,4,8,512]{3,2,1,0:T(8,128)S(1)} %get-tuple-element.13), channel_id=1, source_target_pairs={{0,8},{8,16},{16,24},{24,32},{32,40},{40,48},{48,56},{56,64},{64,7... | collective-permute-start | bytes 393224 | tf_op jit(solution)/shard_map/ppermute | solution.py:15
  24.8 13.7 %collective-permute-start.1 = (f32[2,4,8,512]{3,2,1,0:T(8,128)S(1)}, f32[2,4,8,512]{3,2,1,0:T(8,128)S(1)}, u32[]{:S(2)}, u32[]{:S(2)}) collective-permute-start(f32[2,4,8,512]{3,2,1,0:T(8,128)S(1)} %get-tuple-element.14), channel_id=1, source_target_pairs={{8,0},{16,8},{24,16},{32,24},{40,32},{48,40},{56,48},{64,56},{72,6... | collective-permute-start | bytes 393224 | tf_op jit(solution)/shard_map/ppermute | solution.py:16
  39.9 1.9 %copy-start = (s32[16]{0:T(128)S(1)}, s32[16]{0:T(128)}, u32[]{:S(2)}) copy-start(s32[16]{0:T(128)} %param.7) | copy-start | bytes 196
Sparse Core Ops, SparseCore 0:
  41.9 95.2 all-gather.1
where the time goes:
time: 151 us
  waiting for transfers between devices  96 us (64%)
  starting transfers between devices  27.5 us (18%)
  between operations  13.6 us (9%)
  other arithmetic  8.62 us (6%)
  local copies, waits for them, and re-layouts  5.02 us (3%)
    all_gather x1, waiting for transfers between devices, on_device(): every = lax.all_gather(weights, 'tm', axis=0, tiled=True)  95.4 us
    ppermute x2, starting transfers between devices, halo_rows(): after = lax.ppermute(head, 'tile', [(i + 1, i) for i in range(ends)])  23.7 us
    ppermute x2, starting transfers between devices, halo_rows(): before = lax.ppermute(tail, 'tile', [(i, i + 1) for i in range(ends)])  3.83 us
    dot_general x1, other arithmetic, on_device(): jnp.einsum('mvxly,mxly->vxly', perturbations[0], by_member, preferred_ele...  3.17 us
  transfers between devices with their start and end apart: 5, of which 2 were waited for; matrix products, arithmetic and copies ran while one was open for 2% of the time, Pallas kernels for 0%

commit v1 on v0

--- a/solution.py
+++ b/solution.py
@@ -44,7 +44,9 @@
     for sweep_index in range(SWEEPS):
         smooth = jnp.where(keep, weight_sweep(smooth, coef), 0.0)
     weights = smooth[:, width : width + rows].astype(jnp.bfloat16)
-    every = lax.all_gather(weights, "tm", axis=0, tiled=True)
+    every = jnp.concatenate(
+        lax.all_to_all(jnp.stack([weights] * lax.axis_size("tm")), "tm", 0, 0), axis=0
+    )
     by_member = jnp.zeros_like(every).at[owner].set(every)
     member_count = owner.shape[0]
     factor = 1.0 / math.sqrt(member_count - 1)

time: 151 us -> 101 us (0.67)
  the two profiles are of different devices: /device:TPU:2 before, /device:TPU:101 now
where the time goes in v1:
time: 101 us
  waiting for transfers between devices  60.9 us (60%)
  starting transfers between devices  26.6 us (26%)
  other arithmetic  7.98 us (8%)
  local copies, waits for them, and re-layouts  4.95 us (5%)
    all_to_all x1, waiting for transfers between devices, on_device(): lax.all_to_all(jnp.stack([weights] * lax.axis_size('tm')), 'tm', 0, 0)  57.2 us
    all_to_all x1, starting transfers between devices, on_device(): lax.all_to_all(jnp.stack([weights] * lax.axis_size('tm')), 'tm', 0, 0)  12.6 us
    ppermute x2, starting transfers between devices, halo_rows(): before = lax.ppermute(tail, 'tile', [(i, i + 1) for i in range(ends)])  10.2 us
    ppermute x2, starting transfers between devices, halo_rows(): after = lax.ppermute(head, 'tile', [(i + 1, i) for i in range(ends)])  3.84 us
    ppermute x2, waiting for transfers between devices, halo_rows(): after = lax.ppermute(head, 'tile', [(i + 1, i) for i in range(ends)])  3.62 us
    dot_general x1, other arithmetic, on_device(): jnp.einsum('mvxly,mxly->vxly', perturbations[0], by_member, preferred_ele...  3.17 us
  transfers between devices with their start and end apart: 5, of which 2 were waited for; matrix products, arithmetic and copies ran while one was open for 3% of the time, Pallas kernels for 0%

profile of v1, /device:TPU:101, one launch (start us, length us, event | category | flops | bytes accessed | tf_op | source)
XLA Modules:
  0.0 100.6 jit_solution(18037231514869602997)
XLA Ops:
  0.0 0.8 fusion.59
  0.8 5.3 %collective-permute-start.2 = (s32[4,512]{1,0:T(4,128)S(1)}, s32[4,512]{1,0:T(4,128)S(1)}, u32[]{:S(2)}, u32[]{:S(2)}) collective-permute-start(s32[4,512]{1,0:T(4,128)S(1)} %get-tuple-element.15), channel_id=1, source_target_pairs={{0,8},{8,16},{16,24},{24,32},{32,40},{40,48},{48,56},{56,64},{64,7... | collective-permute-start | bytes 24584 | tf_op jit(solution)/shard_map/ppermute | solution.py:15
  6.1 1.9 %collective-permute-start.3 = (s32[4,512]{1,0:T(4,128)S(1)}, s32[4,512]{1,0:T(4,128)S(1)}, u32[]{:S(2)}, u32[]{:S(2)}) collective-permute-start(s32[4,512]{1,0:T(4,128)S(1)} %get-tuple-element.16), channel_id=1, source_target_pairs={{8,0},{16,8},{24,16},{32,24},{40,32},{48,40},{56,48},{64,56},{72,6... | collective-permute-start | bytes 24584 | tf_op jit(solution)/shard_map/ppermute | solution.py:16
  8.0 1.0 fusion.58
  9.0 4.9 %collective-permute-start = (f32[2,4,8,512]{3,2,1,0:T(8,128)S(1)}, f32[2,4,8,512]{3,2,1,0:T(8,128)S(1)}, u32[]{:S(2)}, u32[]{:S(2)}) collective-permute-start(f32[2,4,8,512]{3,2,1,0:T(8,128)S(1)} %get-tuple-element.13), channel_id=1, source_target_pairs={{0,8},{8,16},{16,24},{24,32},{32,40},{40,48},{48,56},{56,64},{64,7... | collective-permute-start | bytes 393224 | tf_op jit(solution)/shard_map/ppermute | solution.py:15
  13.9 1.9 %collective-permute-start.1 = (f32[2,4,8,512]{3,2,1,0:T(8,128)S(1)}, f32[2,4,8,512]{3,2,1,0:T(8,128)S(1)}, u32[]{:S(2)}, u32[]{:S(2)}) collective-permute-start(f32[2,4,8,512]{3,2,1,0:T(8,128)S(1)} %get-tuple-element.14), channel_id=1, source_target_pairs={{8,0},{16,8},{24,16},{32,24},{40,32},{48,40},{56,48},{64,56},{72,6... | collective-permute-start | bytes 393224 | tf_op jit(solution)/shard_map/ppermute | solution.py:16
  15.8 0.8 slice_bitcast_fusion.1
  16.6 0.1 slice.128
  16.7 0.0 collective-permute-done.2
  16.7 0.0 collective-permute-done.3
  16.7 0.7 add_compare_fusion
  17.4 0.1 select_select_fusion
  17.5 0.2 fusion.45
  17.8 0.0 collective-permute-done
  17.8 3.6 %collective-permute-done.1 = f32[2,4,8,512]{3,2,1,0:T(8,128)S(1)} collective-permute-done((f32[2,4,8,512]{3,2,1,0:T(8,128)S(1)}, f32[2,4,8,512]{3,2,1,0:T(8,128)S(1)}, u32[]{:S(2)}, u32[]{:S(2)}) %collective-permute-start.1) | collective-permute-done | bytes 131104 | tf_op jit(solution)/shard_map/ppermute | solution.py:16
  21.4 1.0 %maximum_select_fusion = f32[2,16,8,512]{3,2,1,0:T(8,128)S(1)} fusion(f32[2,4,8,512]{3,2,1,0:T(8,128)S(1)} %collective-permute-done.1, f32[2,8,8,512]{3,2,1,0:T(8,128)} %param.5, f32[2,4,8,512]{3,2,1,0:T(8,128)S(1)} %collective-permute-done, pred[16]{0:T(512)(128)(4,1)S(1)} %compare_and_fusion), kind=kLoop, calls=%fused_computation.63 | loop fusion | flops 393216 | bytes 1048592 | tf_op jit(solution)/shard_map/jit(_where)/select_n | solution.py:43
  22.5 0.4 fusion.6
  22.8 0.4 fusion.19
  23.2 0.4 fusion.32
  23.6 0.0 copy-start
  23.6 0.3 fusion.40
  24.0 0.1 fusion.56
  24.1 1.1 %stack.2 = bf16[8,2,8,8,512]{4,3,2,1,0:T(8,128)(2,1)} broadcast(bf16[2,8,8,512]{3,2,1,0:T(8,128)(2,1)S(1)} %fusion.56), dimensions={1,2,3,4} | broadcast | bytes 1179648 | tf_op jit(solution)/shard_map/stack | solution.py:48
  25.2 12.6 %all-to-all-start = ((bf16[8,2,8,8,512]{4,3,2,1,0:T(8,128)(2,1)}), bf16[8,2,8,8,512]{4,3,2,1,0:T(8,128)(2,1)S(1)}, u32[]{:S(2)}, u32[]{:S(2)}) async-start(bf16[8,2,8,8,512]{4,3,2,1,0:T(8,128)(2,1)} %stack.2), calls=%async_computation | async-start | bytes 2097152 | tf_op jit(solution)/shard_map/all_to_all | solution.py:48
  37.8 0.0 copy-done
  37.8 57.2 %all-to-all-done = bf16[8,2,8,8,512]{4,3,2,1,0:T(8,128)(2,1)S(1)} async-done(((bf16[8,2,8,8,512]{4,3,2,1,0:T(8,128)(2,1)}), bf16[8,2,8,8,512]{4,3,2,1,0:T(8,128)(2,1)S(1)}, u32[]{:S(2)}, u32[]{:S(2)}) %all-to-all-start) | async-done | bytes 1048608 | tf_op jit(solution)/shard_map/all_to_all | solution.py:48
  95.1 0.1 broadcast_in_dim.96
  95.2 1.1 %scatter_fusion = bf16[16,8,8,512]{3,2,1,0:T(8,128)(2,1)S(1)} fusion(bf16[16,8,8,512]{3,2,1,0:T(8,128)(2,1)S(1)} %broadcast_in_dim.96, s32[16]{0:T(128)S(1)} %compare_select_fusion, bf16[16,8,8,512]{3,2,1,0:T(8,128)(2,1)S(1)} %bitcast.15), kind=kCustom, calls=%fused_computation | custom fusion | bytes 3145792 | tf_op jit(solution)/shard_map/scatter | solution.py:50
  96.3 0.3 bitcast_convert_fusion
  96.6 3.2 %multiply_reduce_fusion = f32[8,8,512,4]{2,1,0,3:T(8,128)S(1)} fusion(f32[8,8,512,16]{2,1,0,3:T(8,128)S(1)} %bitcast_convert_fusion, bf16[1,16,4,8,8,512]{5,4,3,2,1,0:T(8,128)(2,1)} %param.6), kind=kLoop, calls=%fused_computation.1 | loop fusion | flops 6160384 | bytes 6815744 | tf_op jit(solution)/shard_map/mvxly,mxly->vxly/dot_general | solution.py:53
  99.8 0.8 multiply_bitcast_fusion
  (4 shorter events, 0.0 us)
Async XLA Ops:
  0.8 15.9 %collective-permute-start.2 = (s32[4,512]{1,0:T(4,128)S(1)}, s32[4,512]{1,0:T(4,128)S(1)}, u32[]{:S(2)}, u32[]{:S(2)}) collective-permute-start(s32[4,512]{1,0:T(4,128)S(1)} %get-tuple-element.15), channel_id=1, source_target_pairs={{0,8},{8,16},{16,24},{24,32},{32,40},{40,48},{48,56},{56,64},{64,7... | collective-permute-start | bytes 24584 | tf_op jit(solution)/shard_map/ppermute | solution.py:15
  6.1 10.6 %collective-permute-start.3 = (s32[4,512]{1,0:T(4,128)S(1)}, s32[4,512]{1,0:T(4,128)S(1)}, u32[]{:S(2)}, u32[]{:S(2)}) collective-permute-start(s32[4,512]{1,0:T(4,128)S(1)} %get-tuple-element.16), channel_id=1, source_target_pairs={{8,0},{16,8},{24,16},{32,24},{40,32},{48,40},{56,48},{64,56},{72,6... | collective-permute-start | bytes 24584 | tf_op jit(solution)/shard_map/ppermute | solution.py:16
  9.0 8.7 %collective-permute-start = (f32[2,4,8,512]{3,2,1,0:T(8,128)S(1)}, f32[2,4,8,512]{3,2,1,0:T(8,128)S(1)}, u32[]{:S(2)}, u32[]{:S(2)}) collective-permute-start(f32[2,4,8,512]{3,2,1,0:T(8,128)S(1)} %get-tuple-element.13), channel_id=1, source_target_pairs={{0,8},{8,16},{16,24},{24,32},{32,40},{40,48},{48,56},{56,64},{64,7... | collective-permute-start | bytes 393224 | tf_op jit(solution)/shard_map/ppermute | solution.py:15
  13.9 7.5 %collective-permute-start.1 = (f32[2,4,8,512]{3,2,1,0:T(8,128)S(1)}, f32[2,4,8,512]{3,2,1,0:T(8,128)S(1)}, u32[]{:S(2)}, u32[]{:S(2)}) collective-permute-start(f32[2,4,8,512]{3,2,1,0:T(8,128)S(1)} %get-tuple-element.14), channel_id=1, source_target_pairs={{8,0},{16,8},{24,16},{32,24},{40,32},{48,40},{56,48},{64,56},{72,6... | collective-permute-start | bytes 393224 | tf_op jit(solution)/shard_map/ppermute | solution.py:16
  23.6 14.2 %copy-start = (s32[16]{0:T(128)S(1)}, s32[16]{0:T(128)}, u32[]{:S(2)}) copy-start(s32[16]{0:T(128)} %param.7) | copy-start | bytes 196
  25.2 69.9 %all-to-all-start = ((bf16[8,2,8,8,512]{4,3,2,1,0:T(8,128)(2,1)}), bf16[8,2,8,8,512]{4,3,2,1,0:T(8,128)(2,1)S(1)}, u32[]{:S(2)}, u32[]{:S(2)}) async-start(bf16[8,2,8,8,512]{4,3,2,1,0:T(8,128)(2,1)} %stack.2), calls=%async_computation | async-start | bytes 2097152 | tf_op jit(solution)/shard_map/all_to_all | solution.py:48
